TPU v7x, 32 devices: a whole 2x2x4 slice. The times are simulated.
32 devices in a mesh: row: 4 (over y, core), col: 8 (over z, x).
Axes of the slice: x: 2, y: 2, z: 4, core: 2. Of those that a mesh axis runs over, the one named last changes fastest.
Arguments:
- left: bfloat16 [128, 8192], P('col', 'row'), may hold values from -6 to 6
- right: bfloat16 [128, 8192], P('row', 'col'), may hold values from -6 to 6
- proj: bfloat16 [1024, 128], replicated, may hold values from -2 to 2
- bias: float32 [128], replicated, may hold values from -1 to 1
- pair_grad: bfloat16 [256, 256, 128], P('row', 'col'), may hold values from -0.1875 to 0.1875
Outputs:
- pair_out: bfloat16 [256, 256, 128], P('row', 'col')
- left_grad: float32 [128, 8192], P('col', 'row')
- right_grad: float32 [128, 8192], P('row', 'col')
- proj_grad: float32 [1024, 128], replicated
All inputs are finite; a program needn't handle non-finite values.
Results may differ from a plain program's by a relative error of at most 0.0056.
Values may be sent and summed in bfloat16 or wider, within the bound.
A program may use at most 128 MiB of HBM per device.

v0:
```python
import jax
import jax.numpy as jnp
from jax import lax
from jax.sharding import PartitionSpec as P

CH = 32
PAIR = 128
SEQS = 128
OUTER = 1024


def shards(left, right, proj, bias, pair_grad):
    left_all = lax.all_gather(left, "col", axis=0, tiled=True)
    right_all = lax.all_gather(right, "row", axis=0, tiled=True)
    seq_count = left_all.shape[0]
    rows_here = left_all.shape[1] // CH
    cols_here = right_all.shape[1] // CH
    left_cube = left_all.reshape(seq_count, rows_here, CH)
    right_cube = right_all.reshape(seq_count, cols_here, CH)
    square = (
        jnp.einsum("sic,sje->ijce", left_cube, right_cube, preferred_element_type=jnp.float32)
        / SEQS
    )
    outers = square.astype(jnp.bfloat16).reshape(rows_here * cols_here, OUTER)
    preact = jnp.dot(outers, proj, preferred_element_type=jnp.float32) + bias
    active = jnp.maximum(preact, 0.0)
    pair_out = (active * active).astype(jnp.bfloat16).reshape(rows_here, cols_here, PAIR)
    grad_pre = (
        pair_grad.reshape(rows_here * cols_here, PAIR).astype(jnp.float32) * 2.0 * active
    ).astype(jnp.bfloat16)
    weight_term = lax.dot_general(
        outers, grad_pre, (((0,), (0,)), ((), ())), preferred_element_type=jnp.float32
    )
    proj_grad = lax.psum(weight_term, ("row", "col"))
    grad_outer = jnp.dot(grad_pre, proj.T, preferred_element_type=jnp.float32).astype(jnp.bfloat16)
    grad_cube = grad_outer.reshape(rows_here, cols_here, CH, CH)
    left_whole = (
        jnp.einsum("ijce,sje->sic", grad_cube, right_cube, preferred_element_type=jnp.float32)
        / SEQS
    )
    right_whole = (
        jnp.einsum("ijce,sic->sje", grad_cube, left_cube, preferred_element_type=jnp.float32) / SEQS
    )
    left_grad = lax.psum_scatter(
        left_whole.reshape(seq_count, rows_here * CH), "col", scatter_dimension=0, tiled=True
    )
    right_grad = lax.psum_scatter(
        right_whole.reshape(seq_count, cols_here * CH), "row", scatter_dimension=0, tiled=True
    )
    return (pair_out, left_grad, right_grad, proj_grad)


def solution(mesh):
    return jax.shard_map(
        shards,
        mesh=mesh,
        in_specs=(P("col", "row"), P("row", "col"), P(), P(), P("row", "col", None)),
        out_specs=(P("row", "col", None), P("col", "row"), P("row", "col"), P()),
        check_vma=False,
    )
```

profile of v0, /device:TPU:0, one launch (start us, length us, event | category | flops | bytes accessed | tf_op | source)
XLA Modules:
  0.0 248.4 jit_solution(3948851120335303654)
XLA Ops:
  8.0 0.0 copy-start
  8.0 0.0 all-reduce.2.cloned.1.call-start
  8.1 33.4 %all_gather.7 = bf16[128,2048]{1,0:T(8,128)(2,1)S(1)} all-gather(bf16[16,2048]{1,0:T(8,128)(2,1)} %param.5), channel_id=1, replica_groups=mesh['row'=4,'col'=8] {'col'}, dimensions={0}, use_global_device_ids=true | all-gather | bytes 589824 | tf_op jit(solution)/shard_map/all_gather | solution.py:13
  41.4 0.3 copy.26
  41.7 6.0 %all_gather.6 = bf16[128,1024]{1,0:T(8,128)(2,1)S(1)} all-gather(bf16[32,1024]{1,0:T(8,128)(2,1)} %param.6), channel_id=1, replica_groups=mesh['row'=4,'col'=8] {'row'}, dimensions={0}, use_global_device_ids=true | all-gather | bytes 327680 | tf_op jit(solution)/shard_map/all_gather | solution.py:14
  47.7 0.2 copy.25
  47.9 5.6 %fusion = bf16[64,32,32,32]{0,3,2,1:T(8,128)(2,1)} fusion(bf16[128,32,32,1]{0,2,3,1:T(8,128)(2,1)S(1)} %bitcast.50, bf16[128,64,32]{0,2,1:T(8,128)(2,1)S(1)} %bitcast.48), kind=kOutput, calls=%fused_computation.1 | convolution fusion | flops 541065216 | bytes 4980736 | tf_op jit(solution)/shard_map/sic,sje->ijce/dot_general | solution.py:21
  53.5 24.6 %copy.28 = bf16[64,32,32,32]{3,2,1,0:T(8,128)(2,1)} copy(bf16[64,32,32,32]{0,3,2,1:T(8,128)(2,1)} %fusion) | data formatting | bytes 8388608 | tf_op jit(solution)/shard_map/convert_element_type | solution.py:24
  78.1 0.0 copy-start.2
  78.1 0.0 copy-start.3
  78.1 23.3 %reshape.36 = bf16[2048,1024]{1,0:T(8,128)(2,1)} reshape(bf16[64,32,32,32]{3,2,1,0:T(8,128)(2,1)} %copy.28) | data formatting | bytes 8388608 | tf_op jit(solution)/shard_map/reshape | solution.py:24
  101.4 0.0 copy-done.2
  101.4 0.0 copy-start.1
  101.4 0.1 convert_multiply_fusion
  101.6 0.0 copy-done
  101.6 0.0 copy-done.3
  101.6 4.4 %fusion.4 = (bf16[2048,128]{1,0:T(8,128)(2,1)S(1)}, bf16[2048,128]{1,0:T(8,128)(2,1)}) fusion(f32[64,32,128]{2,1,0:T(8,128)S(1)} %convert_multiply_fusion, f32[128]{0:T(128)S(1)} %copy-done.3, bf16[2048,1024]{1,0:T(8,128)(2,1)} %reshape.36, bf16[1024,128]{1,0:T(8,128)(2,1)S(1)} %copy-done), kind=kOutput, calls=%fused_computation.10 | convolution fusion | flops 538443776 | bytes 6554112 | tf_op jit(solution)/shard_map/dot_general | solution.py:25
  106.0 0.0 copy-done.1
  106.0 2.1 fusion.7
  108.1 0.0 all-reduce.2.cloned.1.call-update
  108.1 0.2 reduce-scatter.5.cloned.1.call-start
  108.3 3.2 %convolution_convert_fusion = bf16[2048,1024]{1,0:T(8,128)(2,1)} fusion(bf16[2048,128]{1,0:T(8,128)(2,1)S(1)} %get-tuple-element.4, bf16[1024,128]{1,0:T(8,128)(2,1)S(1)} %copy-done), kind=kOutput, calls=%fused_computation.2 | convolution fusion | flops 538968064 | bytes 4980736 | tf_op jit(solution)/shard_map/dot_general | solution.py:35
  111.5 20.3 %reshape.38 = bf16[64,32,32,32]{3,2,1,0:T(8,128)(2,1)} reshape(bf16[2048,1024]{1,0:T(8,128)(2,1)} %convolution_convert_fusion) | data formatting | bytes 8388608 | tf_op jit(solution)/shard_map/reshape | solution.py:36
  131.9 10.3 %fusion.3 = f32[32,32,128]{2,1,0:T(8,128)S(1)} fusion(bf16[64,32,32,32]{3,2,1,0:T(8,128)(2,1)} %reshape.38, bf16[128,64,32,1]{0,2,3,1:T(8,128)(2,1)S(1)} %bitcast.49), kind=kOutput, calls=%fused_computation.8 | convolution fusion | flops 537001984 | bytes 5242880 | tf_op jit(solution)/shard_map/ijce,sic->sje/dot_general | solution.py:42
  142.2 1.0 copy.31
  143.2 0.0 reduce-scatter.5.cloned.1.call-update
  143.2 0.0 reduce-scatter.3.cloned.1.call-start
  143.3 9.1 %fusion.2 = f32[64,32,128]{2,1,0:T(8,128)S(1)} fusion(bf16[64,32,32,32]{3,2,1,0:T(8,128)(2,1)} %reshape.38, bf16[128,32,32,1]{0,2,1,3:T(8,128)(2,1)S(1)} %bitcast.51), kind=kOutput, calls=%fused_computation.6 | convolution fusion | flops 537133056 | bytes 5505024 | tf_op jit(solution)/shard_map/ijce,sje->sic/dot_general | solution.py:38
  152.4 1.3 copy.29
  153.7 0.0 reduce-scatter.3.cloned.1.call-update
  153.8 85.4 %all-reduce.2.cloned.1.call-done = f32[1024,128]{1,0:T(8,128)} async-done(((f32[1024,128]{1,0:T(8,128)}), f32[1024,128]{1,0:T(8,128)}) %all-reduce.2.cloned.1.call-update) | async-done | bytes 524304 | tf_op jit(solution)/shard_map/psum | solution.py:34
  239.1 0.0 reduce-scatter.5.cloned.1.call-done
  239.1 0.0 reduce-scatter.3.cloned.1.call-done
  239.1 1.9 copy.41
Async XLA Ops:
  8.0 93.6 %copy-start = (bf16[1024,128]{1,0:T(8,128)(2,1)S(1)}, bf16[1024,128]{1,0:T(8,128)(2,1)}, u32[]{:S(2)}) copy-start(bf16[1024,128]{1,0:T(8,128)(2,1)} %param.7) | copy-start | bytes 786436
  8.0 231.1 %all-reduce.2.cloned.1.call-start = ((), (), s32[]{:S(2)}) async-start(), calls=%async_computation.4 | async-start | bytes 1048576 | tf_op jit(solution)/shard_map/psum | solution.py:34
  78.1 23.3 %copy-start.2 = (bf16[64,32,128]{2,1,0:T(8,128)(2,1)S(1)}, bf16[64,32,128]{2,1,0:T(8,128)(2,1)}, u32[]{:S(2)}) copy-start(bf16[64,32,128]{2,1,0:T(8,128)(2,1)} %param.9) | copy-start | bytes 1572868
  78.1 23.5 %copy-start.3 = (f32[128]{0:T(128)S(1)}, f32[128]{0:T(128)}, u32[]{:S(2)}) copy-start(f32[128]{0:T(128)} %param.8) | copy-start | bytes 1540
  101.4 4.5 %copy-start.1 = (bf16[2048,1024]{1,0:T(8,128)(2,1)S(1)}, bf16[2048,1024]{1,0:T(8,128)(2,1)}, u32[]{:S(2)}) copy-start(bf16[2048,1024]{1,0:T(8,128)(2,1)} %reshape.36) | copy-start | bytes 12582916
  108.1 131.0 %reduce-scatter.5.cloned.1.call-start = ((), (), s32[]{:S(2)}) async-start(), calls=%async_computation.3 | async-start | bytes 655360 | tf_op jit(solution)/shard_map/reduce_scatter | solution.py:47
  143.2 95.9 %reduce-scatter.3.cloned.1.call-start = ((), (), s32[]{:S(2)}) async-start(), calls=%async_computation.2 | async-start | bytes 1179648 | tf_op jit(solution)/shard_map/reduce_scatter | solution.py:44
Sparse Core Ops, SparseCore 0:
  108.2 130.8 all-reduce.1
Sparse Core Ops, SparseCore 1:
  143.3 22.7 reduce-scatter.4
  169.9 64.3 reduce-scatter.2
where the time goes:
time: 250 us; the launch traced here: 248 us
  waiting for transfers between devices  85.4 us (34%)
  local copies, waits for them, and re-layouts  72.9 us (29%)
  blocking collectives  39.4 us (16%)
  matrix products  34.8 us (14%)
  between operations  15.5 us (6%)
    psum x1, waiting for transfers between devices, shards(): proj_grad = lax.psum(weight_term, ('row', 'col'))  85.4 us
    all_gather x1, blocking collectives, shards(): left_all = lax.all_gather(left, 'col', axis=0, tiled=True)  33.4 us
    convert_element_type x1, local copies, waits for them, and re-layouts, shards(): outers = square.astype(jnp.bfloat16).reshape(rows_here * cols_here, OUTER)  24.6 us
    reshape x1, local copies, waits for them, and re-layouts, shards(): outers = square.astype(jnp.bfloat16).reshape(rows_here * cols_here, OUTER)  23.3 us
    reshape x1, local copies, waits for them, and re-layouts, shards(): grad_cube = grad_outer.reshape(rows_here, cols_here, CH, CH)  20.3 us
    dot_general x1, matrix products, shards(): jnp.einsum('ijce,sic->sje', grad_cube, left_cube, preferred_element_type=...  10.3 us
    dot_general x1, matrix products, shards(): jnp.einsum('ijce,sje->sic', grad_cube, right_cube, preferred_element_type...  9.14 us
    all_gather x1, blocking collectives, shards(): right_all = lax.all_gather(right, 'row', axis=0, tiled=True)  5.99 us
  transfers between devices with their start and end apart: 3, of which 1 were waited for; matrix products, arithmetic and copies ran while one was open for 18% of the time, Pallas kernels for 0%

commit v1 on v0

v1 whole, which is shorter than its diff:
```python
import functools

import jax
import jax.numpy as jnp
from jax import lax
from jax.experimental import pallas as pl
from jax.experimental.pallas import tpu as pltpu
from jax.sharding import PartitionSpec as P

CH = 32
PAIR = 128
LANES = 128
PACK = LANES // CH
WIDE = PACK * LANES
TILE = 256
MESH = pl.DeviceIdType.MESH
F32 = jnp.float32
BF16 = jnp.bfloat16


def inner_size(n):
    inner = 1
    while inner * inner * 4 <= n and n % (inner * 2) == 0:
        inner *= 2
    return inner


def dot(a, b):
    return jnp.dot(a, b, preferred_element_type=F32)


def aligned(index, size):
    return pl.ds(pl.multiple_of(index * size, size), size)


def kernel(
    R, C, share,
    left, right, proj, bias, pair_grad,
    pair_out, left_out, right_out, proj_out,
    lbuf, rbuf, lfull, ltrans, rtrans, rperm_t, rperm,
    pfull, spread, spread_t, outer, gpre, gpre_t, gouter,
    pterm, psend, precv, psum, pshare, pparts, pgather,
    rtmp, rown, rsend, rparts, lown, lsend, lxparts, lzsend, lzparts,
    s_lz, r_lz, s_lx, r_lx, s_rg, r_rg,
    s_pc, r_pc, s_ps, r_ps, s_pa, r_pa, s_pe, r_pe,
    s_rs, r_rs, s_lsx, r_lsx, s_lsz, r_lsz,
):
    C2 = inner_size(C)
    C1 = C // C2
    row, col = lax.axis_index("row"), lax.axis_index("col")
    z, x = col // C2, lax.rem(col, C2)
    seqs = lfull.shape[0]
    lwide = left.shape[1]
    rwide = right.shape[1]
    cols_here = rwide // CH
    groups = lwide // LANES
    rows = groups * cols_here
    scale = 1.0 / seqs

    def send(src, dst, ssem, rsem, to_row, to_col):
        return pltpu.make_async_remote_copy(
            src_ref=src, dst_ref=dst, send_sem=ssem, recv_sem=rsem,
            device_id=(to_row, to_col), device_id_type=MESH,
        )

    def zpeer(d):
        return lax.rem(z + d, C1)

    def xpeer(d):
        return lax.rem(x + d, C2)

    def rpeer(d):
        return lax.rem(row + d, R)

    barrier = pltpu.get_barrier_semaphore()
    for d in range(1, R):
        pl.semaphore_signal(barrier, inc=1, device_id=(rpeer(d), col), device_id_type=MESH)
    for d in range(1, C2):
        pl.semaphore_signal(
            barrier, inc=1, device_id=(row, z * C2 + xpeer(d)), device_id_type=MESH)
    for d in range(1, C1):
        pl.semaphore_signal(
            barrier, inc=1, device_id=(row, zpeer(d) * C2 + x), device_id_type=MESH)
    pl.semaphore_wait(barrier, R - 1 + C1 - 1 + C2 - 1)

    pending = []

    def go(copy):
        copy.start()
        pending.append(copy)
        return copy

    for d in range(1, R):
        go(send(right, rbuf.at[row], s_rg.at[d - 1], r_rg.at[d - 1], rpeer(d), col))
    for d in range(1, C1):
        go(send(left, lbuf.at[col], s_lz.at[d - 1], r_lz.at[d - 1], row, zpeer(d) * C2 + x))
    for d in range(1, C2):
        go(send(left, lbuf.at[col], s_lx.at[d - 1, 0], r_lx.at[d - 1, 0], row, z * C2 + xpeer(d)))

    lbuf[col] = left[...]
    rbuf[row] = right[...]
    pfull[...] = proj[...].astype(F32)
    lane_of = lax.broadcasted_iota(jnp.int32, (LANES, LANES), 1) // CH
    zero = jnp.zeros((CH, LANES), BF16)

    @pl.loop(0, CH)
    def _(e):
        block = pfull[pl.ds(e, CH, stride=CH), :]
        narrow = block.astype(BF16)
        spread[aligned(e, LANES), :] = jnp.concatenate(
            [
                jnp.concatenate([narrow if a == b else zero for b in range(PACK)], axis=1)
                for a in range(PACK)
            ],
            axis=0,
        )
        turned = jnp.concatenate([block] * PACK, axis=0).T
        for a in range(PACK):
            spread_t[a * LANES:(a + 1) * LANES, aligned(e, LANES)] = jnp.where(
                lane_of == a, turned, 0.0
            ).astype(BF16)

    for d in range(1, C1):
        block = lax.rem(z + C1 - d, C1) * C2 + x
        send(left, lbuf.at[block], s_lz.at[d - 1], r_lz.at[d - 1], row, col).wait_recv()
        for k in range(1, C2):
            go(send(
                lbuf.at[block], lbuf.at[block], s_lx.at[k - 1, d], r_lx.at[k - 1, d],
                row, z * C2 + xpeer(k)))
    for d in range(1, R):
        source = lax.rem(row + R - d, R)
        send(right, rbuf.at[source], s_rg.at[d - 1], r_rg.at[d - 1], row, col).wait_recv()

    rtrans[...] = rbuf[...].astype(F32).reshape(seqs, rwide).T

    @pl.loop(0, CH)
    def _(e):
        rperm_t[aligned(e, cols_here), :] = rtrans[
            pl.ds(e, cols_here, stride=CH), :].astype(BF16)

    rperm[...] = rperm_t[...].astype(F32).T.astype(BF16)

    for d in range(C1):
        for k in range(1, C2):
            block = lax.rem(z + C1 - d, C1) * C2 + lax.rem(x + C2 - k, C2)
            send(left, lbuf.at[block], s_lx.at[k - 1, d], r_lx.at[k - 1, d], row, col).wait_recv()
    whole_left = lbuf[...].astype(F32).reshape(seqs, lwide)
    lfull[...] = whole_left.astype(BF16)

    @pl.loop(0, lwide // TILE)
    def _(t):
        part = (dot(rperm_t[...], lfull[:, aligned(t, TILE)]) * scale).astype(BF16)
        for h in range(TILE // LANES):
            for e in range(CH):
                outer[aligned(t * (TILE // LANES) + h, cols_here), e * LANES:(e + 1) * LANES] = (
                    part[e * cols_here:(e + 1) * cols_here, h * LANES:(h + 1) * LANES])

    wide_bias = jnp.concatenate([bias[...]] * PACK, axis=1)

    @pl.loop(0, rows // TILE)
    def _(t):
        preact = dot(outer[aligned(t, TILE), :], spread[...]) + wide_bias
        active = jnp.maximum(preact, 0.0)
        square = (active * active).astype(BF16)
        per = TILE // cols_here
        for g in range(per):
            for a in range(PACK):
                token = (t * per + g) * PACK + a
                here = slice(g * cols_here, (g + 1) * cols_here)
                there = slice(a * LANES, (a + 1) * LANES)
                pair_out[token] = square[here, there]
                gpre[aligned(t * per + g, cols_here), there] = (
                    pair_grad[token].astype(F32) * 2.0 * active[here, there]).astype(BF16)
        gpre_t[:, aligned(t, TILE)] = gpre[aligned(t, TILE), :].astype(F32).T.astype(BF16)

    @pl.loop(0, CH * LANES // TILE)
    def _(t):
        part = dot(gpre_t[...], outer[:, aligned(t, TILE)])
        for h in range(TILE // LANES):
            lanes = slice(h * LANES, (h + 1) * LANES)
            picked = part[:LANES, lanes]
            for a in range(1, PACK):
                picked = jnp.where(lane_of == a, part[a * LANES:(a + 1) * LANES, lanes], picked)
            turned = picked.T
            total = turned[:CH]
            for a in range(1, PACK):
                total = total + turned[a * CH:(a + 1) * CH]
            pterm[aligned(t * (TILE // LANES) + h, CH), :] = total

    if share:
        half = pterm.shape[0] // 2
        core = lax.rem(row, 2)
        other = row + 1 - 2 * core
        count = half // share
        me = (row // 2) * C + col
        mine = pterm[aligned(core, half), :]
        psend[...] = pterm[aligned(1 - core, half), :].astype(BF16)
        swap = go(send(psend, precv, s_pc, r_pc, other, col))

    @pl.loop(0, CH * LANES // TILE)
    def _(t):
        part = dot(gpre[...], spread_t[:, aligned(t, TILE)]).astype(BF16)
        for h in range(TILE // LANES):
            for g in range(groups):
                gouter[aligned(t * (TILE // LANES) + h, cols_here), g * LANES:(g + 1) * LANES] = (
                    part[g * cols_here:(g + 1) * cols_here, h * LANES:(h + 1) * LANES])

    if share:
        def owner(k):
            return (k // C) * 2 + core, lax.rem(k, C)

        swap.wait_recv()
        both = (pterm[aligned(core, half), :] + precv[...].astype(F32)).reshape(count, share, PAIR)
        psum[...] = both
        pshare[...] = both.astype(BF16)
        scatter = []
        for d in range(1, count):
            k = lax.rem(me + d, count)
            scatter.append(go(send(
                pshare.at[k], pparts.at[d - 1], s_ps.at[d - 1], r_ps.at[d - 1], *owner(k))))

    @pl.loop(0, lwide // TILE)
    def _(t):
        part = (dot(rperm[...], gouter[:, aligned(t, TILE)]) * scale).reshape(
            C, seqs // C, TILE)
        lown[:, :, aligned(t, TILE)] = part
        lsend[:, :, aligned(t, TILE)] = part.astype(BF16)

    inner = []
    for k in range(1, C2):
        for d in list(range(1, C1)) + [0]:
            inner.append(go(send(
                lsend.at[zpeer(d) * C2 + xpeer(k)], lxparts.at[k - 1, d],
                s_lsx.at[k - 1, d], r_lsx.at[k - 1, d], row, z * C2 + xpeer(k))))

    ltrans[...] = lfull[...].astype(F32).T.astype(BF16)

    @pl.loop(0, CH * cols_here // TILE)
    def _(t):
        part = dot(gouter[aligned(t, TILE), :], ltrans[...]) * scale
        per = TILE // cols_here
        for k in range(per):
            rtmp[pl.ds(t * per + k, cols_here, stride=CH), :] = (
                part[k * cols_here:(k + 1) * cols_here])

    turned = rtmp[...].T.reshape(R, seqs // R, rwide)
    rown[...] = turned
    rsend[...] = turned.astype(BF16)
    rights = [
        go(send(rsend.at[rpeer(d)], rparts.at[d - 1], s_rs.at[d - 1], r_rs.at[d - 1], rpeer(d), col))
        for d in range(1, R)
    ]

    if share:
        for copy in scatter:
            copy.wait_recv()
        total = psum[me]
        for d in range(1, count):
            total = total + pparts[d - 1].astype(F32)
        pgather[core, me] = total.astype(BF16)
        for d in range(1, count):
            k = lax.rem(me + d, count)
            go(send(
                pgather.at[core, me], pgather.at[core, me], s_pa.at[d - 1], r_pa.at[d - 1],
                *owner(k)))
    else:
        proj_out[...] = pterm[...]

    for copy in inner:
        copy.wait_recv()
    outers = []
    for d in range(1, C1):
        total = lown[zpeer(d) * C2 + x]
        for k in range(1, C2):
            total = total + lxparts[k - 1, d].astype(F32)
        lzsend[d - 1] = total.astype(BF16)
        outers.append(go(send(
            lzsend.at[d - 1], lzparts.at[d - 1], s_lsz.at[d - 1], r_lsz.at[d - 1],
            row, zpeer(d) * C2 + x)))

    for copy in rights:
        copy.wait_recv()
    total = rown[row]
    for d in range(1, R):
        total = total + rparts[d - 1].astype(F32)
    right_out[...] = total

    if share:
        for d in range(1, count):
            k = lax.rem(me + count - d, count)
            send(
                pgather.at[core, me], pgather.at[core, k], s_pa.at[d - 1], r_pa.at[d - 1],
                *owner(k)).wait_recv()
        swap = go(send(pgather.at[core], pgather.at[core], s_pe, r_pe, other, col))

    total = lown[col]
    for k in range(1, C2):
        total = total + lxparts[k - 1, 0].astype(F32)
    for d, copy in enumerate(outers):
        copy.wait_recv()
        total = total + lzparts[d].astype(F32)
    left_out[...] = total

    if share:
        send(pgather.at[core], pgather.at[1 - core], s_pe, r_pe, other, col).wait_recv()
        rtmp_rows = pgather[...].astype(F32).reshape(2 * half, PAIR)
        pfull[...] = rtmp_rows

        @pl.loop(0, CH)
        def _(e):
            proj_out[pl.ds(e, CH, stride=CH), :] = pfull[aligned(e, CH), :]

    for copy in pending:
        copy.wait_send()


def solution(mesh):
    R, C = mesh.shape["row"], mesh.shape["col"]

    def step(left, right, proj, bias, pair_grad):
        lseq, lwide = left.shape
        rseq, rwide = right.shape
        seqs = lseq * C
        outer_size = proj.shape[0]
        cols_here = rwide // CH
        rows = lwide // LANES * cols_here
        C2 = inner_size(C)
        C1 = C // C2
        share = outer_size // (R * C) if R % 2 == 0 else 0
        if share % 16:
            share = 0
        half = outer_size // 2
        keep = share or half
        count = half // keep
        some = max(count - 1, 1)
        dma = pltpu.SemaphoreType.DMA
        V = pltpu.VMEM
        scratch = [
            V((C, lseq, lwide), BF16), V((R, rseq, rwide), BF16), V((seqs, lwide), BF16),
            V((lwide, seqs), BF16), V((rwide, seqs), F32), V((rwide, seqs), BF16),
            V((seqs, rwide), BF16),
            V((outer_size, PAIR), F32), V((PACK * outer_size, WIDE), BF16),
            V((WIDE, PACK * outer_size), BF16), V((rows, PACK * outer_size), BF16),
            V((rows, WIDE), BF16), V((WIDE, rows), BF16), V((rwide, lwide), BF16),
            V((outer_size, PAIR), F32), V((half, PAIR), BF16), V((half, PAIR), BF16),
            V((count, keep, PAIR), F32), V((count, keep, PAIR), BF16),
            V((some, keep, PAIR), BF16), V((2, count, keep, PAIR), BF16),
            V((rwide, seqs), F32), V((R, rseq, rwide), F32), V((R, rseq, rwide), BF16),
            V((R - 1, rseq, rwide), BF16),
            V((C, lseq, lwide), F32), V((C, lseq, lwide), BF16),
            V((C2 - 1, C1, lseq, lwide), BF16), V((C1 - 1, lseq, lwide), BF16),
            V((C1 - 1, lseq, lwide), BF16),
            dma((C1 - 1,)), dma((C1 - 1,)), dma((C2 - 1, C1)), dma((C2 - 1, C1)),
            dma((R - 1,)), dma((R - 1,)),
            dma, dma, dma((some,)), dma((some,)), dma((some,)), dma((some,)), dma, dma,
            dma((R - 1,)), dma((R - 1,)), dma((C2 - 1, C1)), dma((C2 - 1, C1)),
            dma((C1 - 1,)), dma((C1 - 1,)),
        ]
        vmem = pl.BlockSpec(memory_space=pltpu.VMEM)
        pair_out, left_grad, right_grad, proj_grad = pl.pallas_call(
            functools.partial(kernel, R, C, share),
            out_shape=(
                jax.ShapeDtypeStruct(pair_grad.shape, BF16),
                jax.ShapeDtypeStruct(left.shape, F32),
                jax.ShapeDtypeStruct(right.shape, F32),
                jax.ShapeDtypeStruct(proj.shape, F32),
            ),
            in_specs=[vmem] * 5,
            out_specs=[vmem] * 4,
            scratch_shapes=scratch,
            compiler_params=pltpu.CompilerParams(
                collective_id=0, has_side_effects=True, vmem_limit_bytes=60 << 20),
        )(left, right, proj, bias.reshape(1, -1), pair_grad)
        if not share:
            proj_grad = proj_grad.reshape(CH, CH, PAIR).transpose(1, 0, 2).reshape(proj.shape)
            proj_grad = lax.psum(proj_grad, ("row", "col"))
        return pair_out, left_grad, right_grad, proj_grad

    return jax.shard_map(
        step,
        mesh=mesh,
        in_specs=(P("col", "row"), P("row", "col"), P(), P(), P("row", "col", None)),
        out_specs=(P("row", "col", None), P("col", "row"), P("row", "col"), P()),
        check_vma=False,
    )
```

time: 250 us -> 55.7 us (0.22)
  waiting for transfers between devices: 85.4 us -> 0 us
  local copies, waits for them, and re-layouts: 72.9 us -> 4.34 us
  Pallas kernels: 0 us -> 50.5 us
  blocking collectives: 39.4 us -> 0 us
  matrix products: 34.8 us -> 0 us
  between operations: 15.5 us -> 0.66 us
    psum x1 -> x0, waiting for transfers between devices: 85.4 us -> none  [shards(): proj_grad = lax.psum(weight_term, ('row', 'col'))]
    pallas_call x0 -> x1, Pallas kernels: none -> 50.5 us  [step(): pl.pallas_call(functools.partial(kernel, R, C, share), out_shape=(jax.Sha...]
    reshape x4 -> x0, local copies, waits for them, and re-layouts: 45.9 us -> none  [the longest x1 23.3 us: shards(): outers = square.astype(jnp.bfloat16).reshape(rows_here * cols_here, OUTER)]
    all_gather x2 -> x0, blocking collectives: 39.4 us -> none  [the longest x1 33.4 us: shards(): left_all = lax.all_gather(left, 'col', axis=0, tiled=True)]
    dot_general x6 -> x0, matrix products: 34.8 us -> none  [the longest x1 10.3 us: shards(): jnp.einsum('ijce,sic->sje', grad_cube, left_cube, preferred_element_type=...]
    convert_element_type x1 -> x0, local copies, waits for them, and re-layouts: 24.6 us -> none  [shards(): outers = square.astype(jnp.bfloat16).reshape(rows_here * cols_here, OUTER)]
  transfers between devices with their start and end apart: 3 -> 0, of which waited for: 1 -> 0; matrix products, arithmetic and copies ran while one was open for 18% -> 0% of each run, Pallas kernels for 0% -> 0%
where the time goes in v1:
time: 55.7 us; the launch traced here: 55.5 us
  Pallas kernels  50.5 us (91%)
  local copies, waits for them, and re-layouts  4.34 us (8%)
  between operations  0.66 us (1%)
    pallas_call x1, Pallas kernels, step(): pl.pallas_call(functools.partial(kernel, R, C, share), out_shape=(jax.Sha...  50.5 us
    unnamed x10, local copies, waits for them, and re-layouts  4.34 us

profile of v1, /device:TPU:0, one launch (start us, length us, event | category | flops | bytes accessed | tf_op | source)
XLA Modules:
  0.0 55.5 jit_solution(4482491766589356817)
XLA Ops:
  0.6 50.5 %shard_map.84 = (bf16[64,32,128]{2,1,0:T(8,128)(2,1)}, f32[16,2048]{1,0:T(8,128)}, f32[32,1024]{1,0:T(8,128)}, f32[1024,128]{1,0:T(8,128)}) custom-call(bf16[16,2048]{1,0:T(8,128)(2,1)} %left.1, bf16[32,1024]{1,0:T(8,128)(2,1)} %right.1, bf16[1024,128]{1,0:T(8,128)(2,1)} %proj.1, f32[1,128]{1,0:T(1,128)} %bitcast.1, bf16[64,32,128]{2,1,0:T(8,128)(2,1)} %pair_grad.1), custom_call_target="tpu_custom_call" | custom-call | tf_op jit(solution)/shard_map/pallas_call | solution.py:360
  51.2 0.0 copy-start.2
  51.2 0.0 copy-start
  51.2 1.9 %copy.13 = bf16[64,32,128]{2,1,0:T(8,128)(2,1)} copy(bf16[64,32,128]{2,1,0:T(8,128)(2,1)} %get-tuple-element.8) | data formatting | bytes 1048576
  53.1 0.0 copy-done.2
  53.1 0.0 copy-start.1
  53.1 0.7 %copy.14 = f32[16,2048]{1,0:T(8,128)} copy(f32[16,2048]{1,0:T(8,128)S(1)} %copy-done.2) | data formatting | bytes 262144
  53.8 0.3 copy-done.1
  54.1 0.7 %copy.15 = f32[32,1024]{1,0:T(8,128)} copy(f32[32,1024]{1,0:T(8,128)S(1)} %copy-done.1) | data formatting | bytes 262144
  54.7 0.0 copy-done
  54.7 0.8 %copy.16 = f32[1024,128]{1,0:T(8,128)} copy(f32[1024,128]{1,0:T(8,128)S(1)} %copy-done) | data formatting | bytes 1048576
Async XLA Ops:
  51.2 2.0 %copy-start.2 = (f32[16,2048]{1,0:T(8,128)S(1)}, f32[16,2048]{1,0:T(8,128)}, u32[]{:S(2)}) copy-start(f32[16,2048]{1,0:T(8,128)} %get-tuple-element.9) | copy-start | bytes 393220
  51.2 3.6 %copy-start = (f32[1024,128]{1,0:T(8,128)S(1)}, f32[1024,128]{1,0:T(8,128)}, u32[]{:S(2)}) copy-start(f32[1024,128]{1,0:T(8,128)} %get-tuple-element.11) | copy-start | bytes 1572868
  53.1 1.0 %copy-start.1 = (f32[32,1024]{1,0:T(8,128)S(1)}, f32[32,1024]{1,0:T(8,128)}, u32[]{:S(2)}) copy-start(f32[32,1024]{1,0:T(8,128)} %get-tuple-element.10) | copy-start | bytes 393220

commit v2 on v1

--- a/solution.py
+++ b/solution.py
@@ -13,6 +13,8 @@
 PACK = LANES // CH
 WIDE = PACK * LANES
 TILE = 256
+LONG = 512
+PARTS = 2
 MESH = pl.DeviceIdType.MESH
 F32 = jnp.float32
 BF16 = jnp.bfloat16
@@ -90,14 +92,23 @@
         pending.append(copy)
         return copy
 
-    for d in range(1, R):
-        go(send(right, rbuf.at[row], s_rg.at[d - 1], r_rg.at[d - 1], rpeer(d), col))
-    for d in range(1, C1):
-        go(send(left, lbuf.at[col], s_lz.at[d - 1], r_lz.at[d - 1], row, zpeer(d) * C2 + x))
-    for d in range(1, C2):
-        go(send(left, lbuf.at[col], s_lx.at[d - 1, 0], r_lx.at[d - 1, 0], row, z * C2 + xpeer(d)))
-
-    lbuf[col] = left[...]
+    lchunk = lwide // PARTS
+    for p in range(PARTS):
+        piece = left.at[:, p * lchunk:(p + 1) * lchunk]
+        for d in range(1, C1):
+            go(send(
+                piece, lbuf.at[p, col], s_lz.at[p, d - 1], r_lz.at[p, d - 1],
+                row, zpeer(d) * C2 + x))
+        for d in range(1, C2):
+            go(send(
+                piece, lbuf.at[p, col], s_lx.at[p, d - 1, 0], r_lx.at[p, d - 1, 0],
+                row, z * C2 + xpeer(d)))
+        if p == 0:
+            for d in range(1, R):
+                go(send(right, rbuf.at[row], s_rg.at[d - 1], r_rg.at[d - 1], rpeer(d), col))
+
+    for p in range(PARTS):
+        lbuf[p, col] = left[:, p * lchunk:(p + 1) * lchunk]
     rbuf[row] = right[...]
     pfull[...] = proj[...].astype(F32)
     lane_of = lax.broadcasted_iota(jnp.int32, (LANES, LANES), 1) // CH
@@ -120,13 +131,28 @@
                 lane_of == a, turned, 0.0
             ).astype(BF16)
 
-    for d in range(1, C1):
-        block = lax.rem(z + C1 - d, C1) * C2 + x
-        send(left, lbuf.at[block], s_lz.at[d - 1], r_lz.at[d - 1], row, col).wait_recv()
-        for k in range(1, C2):
-            go(send(
-                lbuf.at[block], lbuf.at[block], s_lx.at[k - 1, d], r_lx.at[k - 1, d],
-                row, z * C2 + xpeer(k)))
+    def pass_on(p):
+        for d in range(1, C1):
+            block = lax.rem(z + C1 - d, C1) * C2 + x
+            send(
+                lbuf.at[p, block], lbuf.at[p, block], s_lz.at[p, d - 1], r_lz.at[p, d - 1],
+                row, col).wait_recv()
+            for k in range(1, C2):
+                go(send(
+                    lbuf.at[p, block], lbuf.at[p, block], s_lx.at[p, k - 1, d],
+                    r_lx.at[p, k - 1, d], row, z * C2 + xpeer(k)))
+
+    def arrive(p):
+        for d in range(C1):
+            for k in range(1, C2):
+                block = lax.rem(z + C1 - d, C1) * C2 + lax.rem(x + C2 - k, C2)
+                send(
+                    lbuf.at[p, block], lbuf.at[p, block], s_lx.at[p, k - 1, d],
+                    r_lx.at[p, k - 1, d], row, col).wait_recv()
+        lfull[:, p * lchunk:(p + 1) * lchunk] = (
+            lbuf[p].astype(F32).reshape(seqs, lchunk).astype(BF16))
+
+    pass_on(0)
     for d in range(1, R):
         source = lax.rem(row + R - d, R)
         send(right, rbuf.at[source], s_rg.at[d - 1], r_rg.at[d - 1], row, col).wait_recv()
@@ -140,43 +166,43 @@
 
     rperm[...] = rperm_t[...].astype(F32).T.astype(BF16)
 
-    for d in range(C1):
-        for k in range(1, C2):
-            block = lax.rem(z + C1 - d, C1) * C2 + lax.rem(x + C2 - k, C2)
-            send(left, lbuf.at[block], s_lx.at[k - 1, d], r_lx.at[k - 1, d], row, col).wait_recv()
-    whole_left = lbuf[...].astype(F32).reshape(seqs, lwide)
-    lfull[...] = whole_left.astype(BF16)
-
-    @pl.loop(0, lwide // TILE)
+    wide_bias = jnp.concatenate([bias[...]] * PACK, axis=1)
+    per = TILE // cols_here
+    share_rows = rows // PARTS
+
+    for p in range(PARTS):
+        arrive(p)
+        if p + 1 < PARTS:
+            pass_on(p + 1)
+
+        @pl.loop(p * lchunk // LONG, (p + 1) * lchunk // LONG)
+        def _(t):
+            part = (dot(rperm_t[...], lfull[:, aligned(t, LONG)]) * scale).astype(BF16)
+            for h in range(LONG // LANES):
+                for e in range(CH):
+                    outer[
+                        aligned(t * (LONG // LANES) + h, cols_here), e * LANES:(e + 1) * LANES
+                    ] = part[e * cols_here:(e + 1) * cols_here, h * LANES:(h + 1) * LANES]
+
+        @pl.loop(p * share_rows // TILE, (p + 1) * share_rows // TILE)
+        def _(t):
+            preact = dot(outer[aligned(t, TILE), :], spread[...]) + wide_bias
+            active = jnp.maximum(preact, 0.0)
+            square = (active * active).astype(BF16)
+            for g in range(per):
+                for a in range(PACK):
+                    token = (t * per + g) * PACK + a
+                    here = slice(g * cols_here, (g + 1) * cols_here)
+                    there = slice(a * LANES, (a + 1) * LANES)
+                    pair_out[token] = square[here, there]
+                    gpre[aligned(t * per + g, cols_here), there] = (
+                        pair_grad[token].astype(F32) * 2.0 * active[here, there]).astype(BF16)
+            gpre_t[:, aligned(t, TILE)] = gpre[aligned(t, TILE), :].astype(F32).T.astype(BF16)
+
+    @pl.loop(0, CH * LANES // LONG)
     def _(t):
-        part = (dot(rperm_t[...], lfull[:, aligned(t, TILE)]) * scale).astype(BF16)
-        for h in range(TILE // LANES):
-            for e in range(CH):
-                outer[aligned(t * (TILE // LANES) + h, cols_here), e * LANES:(e + 1) * LANES] = (
-                    part[e * cols_here:(e + 1) * cols_here, h * LANES:(h + 1) * LANES])
-
-    wide_bias = jnp.concatenate([bias[...]] * PACK, axis=1)
-
-    @pl.loop(0, rows // TILE)
-    def _(t):
-        preact = dot(outer[aligned(t, TILE), :], spread[...]) + wide_bias
-        active = jnp.maximum(preact, 0.0)
-        square = (active * active).astype(BF16)
-        per = TILE // cols_here
-        for g in range(per):
-            for a in range(PACK):
-                token = (t * per + g) * PACK + a
-                here = slice(g * cols_here, (g + 1) * cols_here)
-                there = slice(a * LANES, (a + 1) * LANES)
-                pair_out[token] = square[here, there]
-                gpre[aligned(t * per + g, cols_here), there] = (
-                    pair_grad[token].astype(F32) * 2.0 * active[here, there]).astype(BF16)
-        gpre_t[:, aligned(t, TILE)] = gpre[aligned(t, TILE), :].astype(F32).T.astype(BF16)
-
-    @pl.loop(0, CH * LANES // TILE)
-    def _(t):
-        part = dot(gpre_t[...], outer[:, aligned(t, TILE)])
-        for h in range(TILE // LANES):
+        part = dot(gpre_t[...], outer[:, aligned(t, LONG)])
+        for h in range(LONG // LANES):
             lanes = slice(h * LANES, (h + 1) * LANES)
             picked = part[:LANES, lanes]
             for a in range(1, PACK):
@@ -185,7 +211,7 @@
             total = turned[:CH]
             for a in range(1, PACK):
                 total = total + turned[a * CH:(a + 1) * CH]
-            pterm[aligned(t * (TILE // LANES) + h, CH), :] = total
+            pterm[aligned(t * (LONG // LANES) + h, CH), :] = total
 
     if share:
         half = pterm.shape[0] // 2
@@ -197,48 +223,58 @@
         psend[...] = pterm[aligned(1 - core, half), :].astype(BF16)
         swap = go(send(psend, precv, s_pc, r_pc, other, col))
 
-    @pl.loop(0, CH * LANES // TILE)
-    def _(t):
-        part = dot(gpre[...], spread_t[:, aligned(t, TILE)]).astype(BF16)
-        for h in range(TILE // LANES):
-            for g in range(groups):
-                gouter[aligned(t * (TILE // LANES) + h, cols_here), g * LANES:(g + 1) * LANES] = (
-                    part[g * cols_here:(g + 1) * cols_here, h * LANES:(h + 1) * LANES])
-
     if share:
         def owner(k):
             return (k // C) * 2 + core, lax.rem(k, C)
 
-        swap.wait_recv()
-        both = (pterm[aligned(core, half), :] + precv[...].astype(F32)).reshape(count, share, PAIR)
-        psum[...] = both
-        pshare[...] = both.astype(BF16)
-        scatter = []
-        for d in range(1, count):
-            k = lax.rem(me + d, count)
-            scatter.append(go(send(
-                pshare.at[k], pparts.at[d - 1], s_ps.at[d - 1], r_ps.at[d - 1], *owner(k))))
-
-    @pl.loop(0, lwide // TILE)
-    def _(t):
-        part = (dot(rperm[...], gouter[:, aligned(t, TILE)]) * scale).reshape(
-            C, seqs // C, TILE)
-        lown[:, :, aligned(t, TILE)] = part
-        lsend[:, :, aligned(t, TILE)] = part.astype(BF16)
-
-    inner = []
-    for k in range(1, C2):
+        def spread_sum():
+            swap.wait_recv()
+            both = (pterm[aligned(core, half), :] + precv[...].astype(F32)).reshape(count, share, PAIR)
+            psum[...] = both
+            pshare[...] = both.astype(BF16)
+            scatter = []
+            for d in range(1, count):
+                k = lax.rem(me + d, count)
+                scatter.append(go(send(
+                    pshare.at[k], pparts.at[d - 1], s_ps.at[d - 1], r_ps.at[d - 1], *owner(k))))
+            return scatter
+
+    chunk_groups = groups // PARTS
+    inner = {}
+    for p in range(PARTS):
+
+        @pl.loop(0, CH * LANES // LONG)
+        def _(t):
+            part = dot(
+                gpre[p * share_rows:(p + 1) * share_rows, :], spread_t[:, aligned(t, LONG)]
+            ).astype(BF16)
+            for h in range(LONG // LANES):
+                for g in range(chunk_groups):
+                    lanes = slice((p * chunk_groups + g) * LANES, (p * chunk_groups + g + 1) * LANES)
+                    gouter[aligned(t * (LONG // LANES) + h, cols_here), lanes] = (
+                        part[g * cols_here:(g + 1) * cols_here, h * LANES:(h + 1) * LANES])
+
+        @pl.loop(0, lchunk // LONG)
+        def _(t):
+            at = aligned(p * (lchunk // LONG) + t, LONG)
+            part = (dot(rperm[...], gouter[:, at]) * scale).reshape(C, seqs // C, LONG)
+            lown[p, :, :, aligned(t, LONG)] = part
+            lsend[p, :, :, aligned(t, LONG)] = part.astype(BF16)
+
         for d in list(range(1, C1)) + [0]:
-            inner.append(go(send(
-                lsend.at[zpeer(d) * C2 + xpeer(k)], lxparts.at[k - 1, d],
-                s_lsx.at[k - 1, d], r_lsx.at[k - 1, d], row, z * C2 + xpeer(k))))
+            for k in range(1, C2):
+                inner[p, d, k] = go(send(
+                    lsend.at[p, zpeer(d) * C2 + xpeer(k)], lxparts.at[p, k - 1, d],
+                    s_lsx.at[p, k - 1, d], r_lsx.at[p, k - 1, d], row, z * C2 + xpeer(k)))
+
+        if p == 0 and share:
+            scatter = spread_sum()
 
     ltrans[...] = lfull[...].astype(F32).T.astype(BF16)
 
     @pl.loop(0, CH * cols_here // TILE)
     def _(t):
         part = dot(gouter[aligned(t, TILE), :], ltrans[...]) * scale
-        per = TILE // cols_here
         for k in range(per):
             rtmp[pl.ds(t * per + k, cols_here, stride=CH), :] = (
                 part[k * cols_here:(k + 1) * cols_here])
@@ -250,6 +286,21 @@
         go(send(rsend.at[rpeer(d)], rparts.at[d - 1], s_rs.at[d - 1], r_rs.at[d - 1], rpeer(d), col))
         for d in range(1, R)
     ]
+
+    outers = {}
+
+    def pass_sums(p):
+        for d in range(1, C1):
+            total = lown[p, zpeer(d) * C2 + x]
+            for k in range(1, C2):
+                inner[p, d, k].wait_recv()
+                total = total + lxparts[p, k - 1, d].astype(F32)
+            lzsend[p, d - 1] = total.astype(BF16)
+            outers[p, d] = go(send(
+                lzsend.at[p, d - 1], lzparts.at[p, d - 1], s_lsz.at[p, d - 1],
+                r_lsz.at[p, d - 1], row, zpeer(d) * C2 + x))
+
+    pass_sums(0)
 
     if share:
         for copy in scatter:
@@ -266,17 +317,8 @@
     else:
         proj_out[...] = pterm[...]
 
-    for copy in inner:
-        copy.wait_recv()
-    outers = []
-    for d in range(1, C1):
-        total = lown[zpeer(d) * C2 + x]
-        for k in range(1, C2):
-            total = total + lxparts[k - 1, d].astype(F32)
-        lzsend[d - 1] = total.astype(BF16)
-        outers.append(go(send(
-            lzsend.at[d - 1], lzparts.at[d - 1], s_lsz.at[d - 1], r_lsz.at[d - 1],
-            row, zpeer(d) * C2 + x)))
+    for p in range(1, PARTS):
+        pass_sums(p)
 
     for copy in rights:
         copy.wait_recv()
@@ -293,13 +335,15 @@
                 *owner(k)).wait_recv()
         swap = go(send(pgather.at[core], pgather.at[core], s_pe, r_pe, other, col))
 
-    total = lown[col]
-    for k in range(1, C2):
-        total = total + lxparts[k - 1, 0].astype(F32)
-    for d, copy in enumerate(outers):
-        copy.wait_recv()
-        total = total + lzparts[d].astype(F32)
-    left_out[...] = total
+    for p in range(PARTS):
+        total = lown[p, col]
+        for k in range(1, C2):
+            inner[p, 0, k].wait_recv()
+            total = total + lxparts[p, k - 1, 0].astype(F32)
+        for d in range(1, C1):
+            outers[p, d].wait_recv()
+            total = total + lzparts[p, d - 1].astype(F32)
+        left_out[:, p * lchunk:(p + 1) * lchunk] = total
 
     if share:
         send(pgather.at[core], pgather.at[1 - core], s_pe, r_pe, other, col).wait_recv()
@@ -326,6 +370,7 @@
         rows = lwide // LANES * cols_here
         C2 = inner_size(C)
         C1 = C // C2
+        lchunk = lwide // PARTS
         share = outer_size // (R * C) if R % 2 == 0 else 0
         if share % 16:
             share = 0
@@ -336,7 +381,7 @@
         dma = pltpu.SemaphoreType.DMA
         V = pltpu.VMEM
         scratch = [
-            V((C, lseq, lwide), BF16), V((R, rseq, rwide), BF16), V((seqs, lwide), BF16),
+            V((PARTS, C, lseq, lchunk), BF16), V((R, rseq, rwide), BF16), V((seqs, lwide), BF16),
             V((lwide, seqs), BF16), V((rwide, seqs), F32), V((rwide, seqs), BF16),
             V((seqs, rwide), BF16),
             V((outer_size, PAIR), F32), V((PACK * outer_size, WIDE), BF16),
@@ -347,14 +392,16 @@
             V((some, keep, PAIR), BF16), V((2, count, keep, PAIR), BF16),
             V((rwide, seqs), F32), V((R, rseq, rwide), F32), V((R, rseq, rwide), BF16),
             V((R - 1, rseq, rwide), BF16),
-            V((C, lseq, lwide), F32), V((C, lseq, lwide), BF16),
-            V((C2 - 1, C1, lseq, lwide), BF16), V((C1 - 1, lseq, lwide), BF16),
-            V((C1 - 1, lseq, lwide), BF16),
-            dma((C1 - 1,)), dma((C1 - 1,)), dma((C2 - 1, C1)), dma((C2 - 1, C1)),
+            V((PARTS, C, lseq, lchunk), F32), V((PARTS, C, lseq, lchunk), BF16),
+            V((PARTS, C2 - 1, C1, lseq, lchunk), BF16), V((PARTS, C1 - 1, lseq, lchunk), BF16),
+            V((PARTS, C1 - 1, lseq, lchunk), BF16),
+            dma((PARTS, C1 - 1)), dma((PARTS, C1 - 1)),
+            dma((PARTS, C2 - 1, C1)), dma((PARTS, C2 - 1, C1)),
             dma((R - 1,)), dma((R - 1,)),
             dma, dma, dma((some,)), dma((some,)), dma((some,)), dma((some,)), dma, dma,
-            dma((R - 1,)), dma((R - 1,)), dma((C2 - 1, C1)), dma((C2 - 1, C1)),
-            dma((C1 - 1,)), dma((C1 - 1,)),
+            dma((R - 1,)), dma((R - 1,)),
+            dma((PARTS, C2 - 1, C1)), dma((PARTS, C2 - 1, C1)),
+            dma((PARTS, C1 - 1)), dma((PARTS, C1 - 1)),
         ]
         vmem = pl.BlockSpec(memory_space=pltpu.VMEM)
         pair_out, left_grad, right_grad, proj_grad = pl.pallas_call(

time: 55.7 us -> 52.1 us (0.935)
  Pallas kernels: 50.5 us -> 46.4 us
    pallas_call x1, Pallas kernels: 50.5 us -> 46.4 us  [step(): pl.pallas_call(functools.partial(kernel, R, C, share), out_shape=(jax.Sha...]
where the time goes in v2:
time: 52.1 us; the launch traced here: 51.4 us
  Pallas kernels  46.4 us (89%)
  local copies, waits for them, and re-layouts  4.34 us (8%)
  between operations  0.66 us (1%)
    pallas_call x1, Pallas kernels, step(): pl.pallas_call(functools.partial(kernel, R, C, share), out_shape=(jax.Sha...  46.4 us
    unnamed x10, local copies, waits for them, and re-layouts  4.34 us

profile of v2, /device:TPU:0, one launch (start us, length us, event | category | flops | bytes accessed | tf_op | source)
XLA Modules:
  0.0 51.4 jit_solution(9568768244992486506)
XLA Ops:
  0.6 46.4 %shard_map.84 = (bf16[64,32,128]{2,1,0:T(8,128)(2,1)}, f32[16,2048]{1,0:T(8,128)}, f32[32,1024]{1,0:T(8,128)}, f32[1024,128]{1,0:T(8,128)}) custom-call(bf16[16,2048]{1,0:T(8,128)(2,1)} %left.1, bf16[32,1024]{1,0:T(8,128)(2,1)} %right.1, bf16[1024,128]{1,0:T(8,128)(2,1)} %proj.1, f32[1,128]{1,0:T(1,128)} %bitcast.1, bf16[64,32,128]{2,1,0:T(8,128)(2,1)} %pair_grad.1), custom_call_target="tpu_custom_call" | custom-call | tf_op jit(solution)/shard_map/pallas_call | solution.py:407
  47.1 0.0 copy-start.2
  47.1 0.0 copy-start
  47.1 1.9 %copy.13 = bf16[64,32,128]{2,1,0:T(8,128)(2,1)} copy(bf16[64,32,128]{2,1,0:T(8,128)(2,1)} %get-tuple-element.8) | data formatting | bytes 1048576
  49.0 0.0 copy-done.2
  49.0 0.0 copy-start.1
  49.0 0.7 %copy.14 = f32[16,2048]{1,0:T(8,128)} copy(f32[16,2048]{1,0:T(8,128)S(1)} %copy-done.2) | data formatting | bytes 262144
  49.7 0.3 copy-done.1
  50.0 0.7 %copy.15 = f32[32,1024]{1,0:T(8,128)} copy(f32[32,1024]{1,0:T(8,128)S(1)} %copy-done.1) | data formatting | bytes 262144
  50.6 0.0 copy-done
  50.6 0.8 %copy.16 = f32[1024,128]{1,0:T(8,128)} copy(f32[1024,128]{1,0:T(8,128)S(1)} %copy-done) | data formatting | bytes 1048576
Async XLA Ops:
  47.1 2.0 %copy-start.2 = (f32[16,2048]{1,0:T(8,128)S(1)}, f32[16,2048]{1,0:T(8,128)}, u32[]{:S(2)}) copy-start(f32[16,2048]{1,0:T(8,128)} %get-tuple-element.9) | copy-start | bytes 393220
  47.1 3.6 %copy-start = (f32[1024,128]{1,0:T(8,128)S(1)}, f32[1024,128]{1,0:T(8,128)}, u32[]{:S(2)}) copy-start(f32[1024,128]{1,0:T(8,128)} %get-tuple-element.11) | copy-start | bytes 1572868
  49.0 1.0 %copy-start.1 = (f32[32,1024]{1,0:T(8,128)S(1)}, f32[32,1024]{1,0:T(8,128)}, u32[]{:S(2)}) copy-start(f32[32,1024]{1,0:T(8,128)} %get-tuple-element.10) | copy-start | bytes 393220
